TPU v7x, 32 devices: a whole 2x2x4 slice. The times are simulated.
32 devices in a mesh: row: 2 (over y), col: 4 (over x, core), tm: 4 (over z).
Axes of the slice: x: 2, y: 2, z: 4, core: 2. Of those that a mesh axis runs over, the one named last changes fastest.
Arguments:
- filled_orbitals: bfloat16 [4, 1024, 1024], P('col', 'row', 'tm'), may hold values from -0.1875 to 0.1875
- empty_orbitals: bfloat16 [4, 1024, 3072], P('col', 'row', 'tm'), may hold values from -0.109375 to 0.109375
- filled_depth: bfloat16 [1024], P('tm'), may hold values from 0.019897461 to 2
- empty_depth: bfloat16 [3072], P('tm'), may hold values from 0.019897461 to 2
- time_points: float32 [4], P('tm'), may hold values from 0.05 to 8
- cosine_weights: float32 [4, 4], replicated, may hold values from -3 to 3
Outputs:
- polar_freq: float32 [4, 4, 1024, 4096], P(None, None, ('row', 'tm'), 'col')
All inputs are finite; a program needn't handle non-finite values.
Results may differ from a plain program's by a relative error of at most 0.0033.
Values may be sent and summed in bfloat16 or wider, within the bound.
No kernel may reach another device: no remote copies, remote signals or barrier semaphores. Data moves between devices by JAX's collectives and lax.ppermute only.
A program may use at most 128 MiB of HBM per device.

v0:
```python
import jax
import jax.numpy as jnp
from jax import lax
from jax.sharding import PartitionSpec as P


def tile_product(left_points, right_points, depths, tau_value):
    band_count = left_points.shape[-1]
    weight_row = jnp.exp(-depths.astype(jnp.float32) * tau_value)
    scaled = (
        right_points.reshape(-1, band_count).astype(jnp.float32) * weight_row[None, :]
    ).astype(jnp.bfloat16)
    return lax.dot_general(
        left_points.reshape(-1, band_count),
        scaled,
        (((1,), (1,)), ((), ())),
        preferred_element_type=jnp.float32,
    )


def on_device(
    filled_orbitals, empty_orbitals, filled_depth, empty_depth, time_points, cosine_weights
):
    tau_value = time_points[0]
    filled_bands, empty_bands, filled_all, empty_all = (
        lax.all_gather(filled_orbitals, "tm", axis=2, tiled=True),
        lax.all_gather(empty_orbitals, "tm", axis=2, tiled=True),
        lax.all_gather(filled_depth, "tm", axis=0, tiled=True),
        lax.all_gather(empty_depth, "tm", axis=0, tiled=True),
    )
    filled_rows, empty_rows = (
        lax.all_gather(filled_bands, "col", axis=0, tiled=True),
        lax.all_gather(empty_bands, "col", axis=0, tiled=True),
    )
    column_filled, column_empty = lax.all_gather(
        (filled_bands, empty_bands), "row", axis=1, tiled=True
    )
    green_filled = tile_product(filled_rows, column_filled, filled_all, tau_value)
    green_empty = tile_product(empty_rows, column_empty, empty_all, tau_value)
    polar_time = (
        (-(green_filled * green_empty))
        .astype(jnp.bfloat16)
        .reshape(filled_rows.shape[0], filled_rows.shape[1], -1)
    )
    return jnp.einsum(
        "ft,tabc->fabc",
        cosine_weights,
        lax.all_to_all(polar_time[None], "tm", split_axis=2, concat_axis=0, tiled=True).astype(
            jnp.float32
        ),
        precision=lax.Precision.HIGHEST,
    )


def solution(mesh):
    in_specs = (P("col", "row", "tm"), P("col", "row", "tm"), P("tm"), P("tm"), P("tm"), P())
    out_specs = P(None, None, ("row", "tm"), "col")
    return jax.shard_map(
        on_device, mesh=mesh, in_specs=in_specs, out_specs=out_specs, check_vma=False
    )
```

profile of v0, /device:TPU:0, one launch (start us, length us, event | category | flops | bytes accessed | tf_op | source)
XLA Modules:
  0.0 491.7 jit_solution(13205183618008928850)
XLA Ops:
  6.5 0.0 copy-start
  6.5 0.0 all-gather.15.cloned.1.call-start
  6.5 0.7 all-gather.15.cloned.1.call-update
  7.3 0.0 all-gather.9.cloned.1.call-start
  7.3 0.7 all-gather.9.cloned.1.call-update
  8.0 0.0 all-gather.17.cloned.1.call-start
  8.1 67.0 %all-gather.15.cloned.1.call-done = bf16[1,512,3072]{2,1,0:T(8,128)(2,1)} async-done(((bf16[1,512,768]{2,1,0:T(8,128)(2,1)}), bf16[1,512,3072]{2,1,0:T(8,128)(2,1)}) %all-gather.15.cloned.1.call-update) | async-done | bytes 3145744 | tf_op jit(solution)/shard_map/all_gather | solution.py:27
  75.1 0.0 copy-start.1
  75.1 0.0 all-gather.17.cloned.1.call-update
  75.1 0.0 all-gather.19.cloned.1.call-start
  75.2 0.5 all-gather.19.cloned.1.call-update
  75.7 0.0 all-gather.11.cloned.1.call-start
  75.8 29.5 %all-gather.9.cloned.1.call-done = bf16[1,512,1024]{2,1,0:T(8,128)(2,1)} async-done(((bf16[1,512,256]{2,1,0:T(8,128)(2,1)}), bf16[1,512,1024]{2,1,0:T(8,128)(2,1)}) %all-gather.9.cloned.1.call-update) | async-done | bytes 1048592 | tf_op jit(solution)/shard_map/all_gather | solution.py:26
  105.3 0.0 all-gather.11.cloned.1.call-update
  105.3 0.0 all-gather.13.cloned.1.call-start
  105.3 0.5 all-gather.13.cloned.1.call-update
  106.5 0.0 copy-done.1
  106.5 0.0 copy-done.2
  106.6 10.1 %all-gather = bf16[4,1,256]{2,1,0:T(2,128)(2,1)S(1)} all-gather(bf16[1,1,256]{2,1,0:T(2,128)(2,1)S(1)} %reshape.26), channel_id=1, replica_groups=mesh['row'=2,'col'=4,'tm'=4] {'tm'}, dimensions={0}, use_global_device_ids=true | all-gather | bytes 2560 | tf_op jit(solution)/shard_map/all_gather | solution.py:28
  116.7 13.1 %all-gather.1 = bf16[4,1,768]{2,1,0:T(2,128)(2,1)S(1)} all-gather(bf16[1,1,768]{2,1,0:T(2,128)(2,1)S(1)} %reshape.28), channel_id=1, replica_groups=mesh['row'=2,'col'=4,'tm'=4] {'tm'}, dimensions={0}, use_global_device_ids=true | all-gather | bytes 7680 | tf_op jit(solution)/shard_map/all_gather | solution.py:29
  129.8 55.7 %all-gather.17.cloned.1.call-done = bf16[1,1024,3072]{2,1,0:T(8,128)(2,1)} async-done(((bf16[1,512,3072]{2,1,0:T(8,128)(2,1)}), bf16[1,1024,3072]{2,1,0:T(8,128)(2,1)}) %all-gather.17.cloned.1.call-update) | async-done | bytes 6291472 | tf_op jit(solution)/shard_map/all_gather | solution.py:35
  185.5 83.5 %all-gather.19.cloned.1.call-done = bf16[4,512,3072]{2,1,0:T(8,128)(2,1)} async-done(((bf16[1,512,3072]{2,1,0:T(8,128)(2,1)}), bf16[4,512,3072]{2,1,0:T(8,128)(2,1)}) %all-gather.19.cloned.1.call-update) | async-done | bytes 12582928 | tf_op jit(solution)/shard_map/all_gather | solution.py:33
  269.0 18.9 %fusion.1 = f32[1024,2048]{1,0:T(8,128)} fusion(bf16[2048,3072]{1,0:T(8,128)(2,1)} %bitcast.35, bf16[1,1024,3072]{2,1,0:T(8,128)(2,1)} %all-gather.17.cloned.1.call-done, f32[3072]{0:T(1024)S(1)} %bitcast.33), kind=kOutput, calls=%fused_computation.3 | convolution fusion | flops 12894339072 | bytes 27275264 | tf_op jit(solution)/shard_map/dot_general | solution.py:13
  287.9 15.6 %all-gather.11.cloned.1.call-done = bf16[1,1024,1024]{2,1,0:T(8,128)(2,1)} async-done(((bf16[1,512,1024]{2,1,0:T(8,128)(2,1)}), bf16[1,1024,1024]{2,1,0:T(8,128)(2,1)}) %all-gather.11.cloned.1.call-update) | async-done | bytes 2097168 | tf_op jit(solution)/shard_map/all_gather | solution.py:35
  303.5 35.9 %all-gather.13.cloned.1.call-done = bf16[4,512,1024]{2,1,0:T(8,128)(2,1)} async-done(((bf16[1,512,1024]{2,1,0:T(8,128)(2,1)}), bf16[4,512,1024]{2,1,0:T(8,128)(2,1)}) %all-gather.13.cloned.1.call-update) | async-done | bytes 4194320 | tf_op jit(solution)/shard_map/all_gather | solution.py:32
  339.4 11.8 %fusion.6 = bf16[2048,1024]{0,1:T(8,128)(2,1)} fusion(f32[1024,2048]{1,0:T(8,128)} %fusion.1, bf16[2048,1024]{1,0:T(8,128)(2,1)} %bitcast.36, bf16[1,1024,1024]{2,1,0:T(8,128)(2,1)} %all-gather.11.cloned.1.call-done, f32[1024]{0:T(1024)S(1)} %bitcast.34), kind=kOutput, calls=%fused_computation.9 | convolution fusion | flops 4304404480 | bytes 18878464 | tf_op jit(solution)/shard_map/dot_general | solution.py:13
  351.2 7.8 %broadcast_in_dim_reshape.3 = bf16[1,4,512,1024]{2,1,3,0:T(4,128)(2,1)} reshape(bf16[2048,1024]{0,1:T(8,128)(2,1)} %fusion.6) | data formatting | bytes 8388608 | tf_op jit(solution)/shard_map/broadcast_in_dim;reshape | solution.py:48
  359.0 10.0 %copy.11 = bf16[1,4,512,1024]{3,1,0,2:T(4,128)(2,1)} copy(bf16[1,4,512,1024]{2,1,3,0:T(4,128)(2,1)} %broadcast_in_dim_reshape.3) | data formatting | bytes 8388608 | tf_op jit(solution)/shard_map/broadcast_in_dim;reshape | solution.py:48
  369.0 98.1 %all_to_all.18 = bf16[1,4,512,1024]{3,1,0,2:T(4,128)(2,1)S(1)} all-to-all(bf16[1,4,512,1024]{3,1,0,2:T(4,128)(2,1)} %copy.11), channel_id=1, replica_groups=mesh['row'=2,'col'=4,'tm'=4] {'tm'}, dimensions={2} | all-to-all | bytes 8388608 | tf_op jit(solution)/shard_map/all_to_all | solution.py:48
  467.2 0.0 copy-done
  467.2 9.4 %convolution_bitcast_fusion = f32[4,4,128,1024]{3,0,2,1:T(4,128)S(1)} fusion(bf16[1,4,4,128,1024]{4,1,3,2,0:T(4,128)(2,1)S(1)} %bitcast.32, f32[4,4]{1,0:T(4,128)S(1)} %copy-done), kind=kOutput, calls=%fused_computation.5 | convolution fusion | flops 100663296 | bytes 12582976 | tf_op jit(solution)/shard_map/ft,tabc->fabc/dot_general | solution.py:45
  476.6 8.3 %copy.14 = f32[4,4,128,1024]{3,2,1,0:T(8,128)} copy(f32[4,4,128,1024]{3,0,2,1:T(4,128)S(1)} %convolution_bitcast_fusion) | data formatting | bytes 16777216 | tf_op jit(solution)/shard_map/ft,tabc->fabc/dot_general | solution.py:45
  (5 shorter events, 0.1 us)
Async XLA Ops:
  6.5 460.6 %copy-start = (f32[4,4]{1,0:T(4,128)S(1)}, f32[4,4]{1,0:T(4,128)}, u32[]{:S(2)}) copy-start(f32[4,4]{1,0:T(4,128)} %param.11) | copy-start | bytes 196
  6.5 68.6 %all-gather.15.cloned.1.call-start = ((), (), s32[]{:S(2)}) async-start(), calls=%async_computation.4 | async-start | bytes 3932160 | tf_op jit(solution)/shard_map/all_gather | solution.py:27
  7.3 98.0 %all-gather.9.cloned.1.call-start = ((), (), s32[]{:S(2)}) async-start(), calls=%async_computation.1 | async-start | bytes 1310720 | tf_op jit(solution)/shard_map/all_gather | solution.py:26
  8.0 177.5 %all-gather.17.cloned.1.call-start = ((), (), s32[]{:S(2)}) async-start(), calls=%async_computation.5 | async-start | bytes 9437184 | tf_op jit(solution)/shard_map/all_gather | solution.py:35
  75.1 31.4 %copy-start.1 = (bf16[768]{0:T(1024)(128)(2,1)S(1)}, bf16[768]{0:T(1024)(128)(2,1)}, u32[]{:S(2)}) copy-start(bf16[768]{0:T(1024)(128)(2,1)} %param.9) | copy-start | bytes 4612
  75.1 31.4 %copy-start.2 = (bf16[256]{0:T(256)(128)(2,1)S(1)}, bf16[256]{0:T(256)(128)(2,1)}, u32[]{:S(2)}) copy-start(bf16[256]{0:T(256)(128)(2,1)} %param.8) | copy-start | bytes 1540
  75.1 193.9 %all-gather.19.cloned.1.call-start = ((), (), s32[]{:S(2)}) async-start(), calls=%async_computation.6 | async-start | bytes 15728640 | tf_op jit(solution)/shard_map/all_gather | solution.py:33
  75.7 227.8 %all-gather.11.cloned.1.call-start = ((), (), s32[]{:S(2)}) async-start(), calls=%async_computation.2 | async-start | bytes 3145728 | tf_op jit(solution)/shard_map/all_gather | solution.py:35
  105.3 234.2 %all-gather.13.cloned.1.call-start = ((), (), s32[]{:S(2)}) async-start(), calls=%async_computation.3 | async-start | bytes 5242880 | tf_op jit(solution)/shard_map/all_gather | solution.py:32
Sparse Core Ops, SparseCore 0:
  8.9 66.1 all-gather.14
  76.7 28.5 all-gather.8
  106.8 78.6 all-gather.16
  186.9 82.0 all-gather.18
  270.4 33.0 all-gather.10
  305.0 34.4 all-gather.12
where the time goes:
time: 492 us
  waiting for transfers between devices  290 us (59%)
  blocking collectives  121 us (25%)
  matrix products  40.1 us (8%)
  local copies, waits for them, and re-layouts  26.1 us (5%)
  between operations  14.2 us (3%)
    all_to_all x1, blocking collectives, on_device(): lax.all_to_all(polar_time[None], 'tm', split_axis=2, concat_axis=0, tiled...  98.1 us
    all_gather x1, waiting for transfers between devices, on_device(): lax.all_gather(empty_bands, 'col', axis=0, tiled=True)  83.5 us
    all_gather x2, waiting for transfers between devices, on_device(): lax.all_gather((filled_bands, empty_bands), 'row', axis=1, tiled=True)  71.3 us
    all_gather x1, waiting for transfers between devices, on_device(): lax.all_gather(empty_orbitals, 'tm', axis=2, tiled=True)  67 us
    all_gather x1, waiting for transfers between devices, on_device(): lax.all_gather(filled_bands, 'col', axis=0, tiled=True)  35.9 us
    dot_general x2, matrix products, tile_product(): lax.dot_general(left_points.reshape(-1, band_count), scaled, (((1,), (1,)...  30.6 us
    all_gather x1, waiting for transfers between devices, on_device(): lax.all_gather(filled_orbitals, 'tm', axis=2, tiled=True)  29.5 us
    another operation x2, local copies, waits for them, and re-layouts, on_device(): polar_time[None]  17.8 us
  transfers between devices with their start and end apart: 6, of which 6 were waited for; matrix products, arithmetic and copies ran while one was open for 4% of the time, Pallas kernels for 0%

commit v1 on v0

--- a/solution.py
+++ b/solution.py
@@ -2,6 +2,32 @@
 import jax.numpy as jnp
 from jax import lax
 from jax.sharding import PartitionSpec as P
+
+
+def bind_domain_in(block_here, pos_dim):
+    aux = list(block_here.shape[1:])
+    aux[pos_dim] *= block_here.shape[0]
+    state_now = jnp.moveaxis(block_here, 0, pos_dim).reshape(aux)
+    return state_now
+
+
+def fields_replace(inputs, across):
+    local_next = inputs[None]
+    dev_n = lax.axis_size(across)
+    for k in range(dev_n.bit_length() - 1):
+        u_next = 1 << k
+        arr_next = tuple(((dd, dd ^ u_next) for dd in range(dev_n)))
+        block_next = lax.ppermute(local_next, axis_name=across, perm=arr_next)
+        n_now = jnp.stack([local_next, block_next], axis=0)
+        y2 = lax.axis_index(across) >> k & 1
+        local_next = jnp.where(y2 == 0, n_now, n_now[::-1]).reshape(-1, *inputs.shape)
+    return local_next
+
+
+def _build_array(a0, z_in, at_axis):
+    taken_in = fields_replace(a0, z_in)
+    b_now = bind_domain_in(taken_in, at_axis)
+    return b_now
 
 
 def tile_product(left_points, right_points, depths, tau_value):
@@ -30,7 +56,7 @@
     )
     filled_rows, empty_rows = (
         lax.all_gather(filled_bands, "col", axis=0, tiled=True),
-        lax.all_gather(empty_bands, "col", axis=0, tiled=True),
+        _build_array(empty_bands, "col", 0),
     )
     column_filled, column_empty = lax.all_gather(
         (filled_bands, empty_bands), "row", axis=1, tiled=True

time: 492 us -> 457 us (0.929)
  waiting for transfers between devices: 290 us -> 228 us
  other arithmetic: 0.04 us -> 23.7 us
    all_gather x1 -> x0, waiting for transfers between devices: 83.5 us -> none  [on_device(): lax.all_gather(empty_bands, 'col', axis=0, tiled=True)]
    ppermute x0 -> x2, waiting for transfers between devices: none -> 80.8 us  [fields_replace(): block_next = lax.ppermute(local_next, axis_name=across, perm=arr_next)]
    all_gather x2, waiting for transfers between devices: 71.3 us -> 0.02 us  [on_device(): lax.all_gather((filled_bands, empty_bands), 'row', axis=1, tiled=True)]
    another operation x0 -> x3, other arithmetic: none -> 15.4 us  [fields_replace(): n_now = jnp.stack([local_next, block_next], axis=0)]
    all_gather x1, waiting for transfers between devices: 35.9 us -> 49.3 us  [on_device(): lax.all_gather(filled_bands, 'col', axis=0, tiled=True)]
    select_n x0 -> x1, other arithmetic: none -> 8.28 us  [fields_replace(): jnp.where(y2 == 0, n_now, n_now[::-1]).reshape(-1, *inputs.shape)]
  transfers between devices with their start and end apart: 6 -> 7, of which waited for: 6 -> 5; matrix products, arithmetic and copies ran while one was open for 4% -> 8% of each run, Pallas kernels for 0% -> 0%
where the time goes in v1:
time: 457 us; the launch traced here: 456 us
  waiting for transfers between devices  228 us (50%)
  blocking collectives  119 us (26%)
  matrix products  41.8 us (9%)
  local copies, waits for them, and re-layouts  27.8 us (6%)
  other arithmetic  23.7 us (5%)
  between operations  14 us (3%)
    all_to_all x1, blocking collectives, on_device(): lax.all_to_all(polar_time[None], 'tm', split_axis=2, concat_axis=0, tiled...  96.6 us
    ppermute x2, waiting for transfers between devices, fields_replace(): block_next = lax.ppermute(local_next, axis_name=across, perm=arr_next)  80.8 us
    all_gather x1, waiting for transfers between devices, on_device(): lax.all_gather(empty_orbitals, 'tm', axis=2, tiled=True)  63.3 us
    all_gather x1, waiting for transfers between devices, on_device(): lax.all_gather(filled_bands, 'col', axis=0, tiled=True)  49.3 us
    all_gather x1, waiting for transfers between devices, on_device(): lax.all_gather(filled_orbitals, 'tm', axis=2, tiled=True)  33.5 us
    dot_general x2, matrix products, tile_product(): lax.dot_general(left_points.reshape(-1, band_count), scaled, (((1,), (1,)...  32.3 us
    another operation x2, local copies, waits for them, and re-layouts, on_device(): polar_time[None]  17.8 us
    another operation x3, other arithmetic, fields_replace(): n_now = jnp.stack([local_next, block_next], axis=0)  15.4 us
  transfers between devices with their start and end apart: 7, of which 5 were waited for; matrix products, arithmetic and copies ran while one was open for 8% of the time, Pallas kernels for 0%

profile of v1, /device:TPU:0, one launch (start us, length us, event | category | flops | bytes accessed | tf_op | source)
XLA Modules:
  0.0 455.8 jit_solution(12240299391068714799)
XLA Ops:
  6.5 0.7 all-gather.8.cloned.1.call-update
  7.3 0.0 all-gather.14.cloned.1.call-start
  7.3 0.7 all-gather.14.cloned.1.call-update
  8.0 0.0 all-gather.10.cloned.1.call-start
  8.1 33.5 %all-gather.8.cloned.1.call-done = bf16[1,512,1024]{2,1,0:T(8,128)(2,1)} async-done(((bf16[1,512,256]{2,1,0:T(8,128)(2,1)}), bf16[1,512,1024]{2,1,0:T(8,128)(2,1)}) %all-gather.8.cloned.1.call-update) | async-done | bytes 1048592 | tf_op jit(solution)/shard_map/all_gather | solution.py:52
  41.6 0.0 all-gather.10.cloned.1.call-update
  41.6 0.0 all-gather.12.cloned.1.call-start
  41.7 63.3 %all-gather.14.cloned.1.call-done = bf16[1,512,3072]{2,1,0:T(8,128)(2,1)} async-done(((bf16[1,512,768]{2,1,0:T(8,128)(2,1)}), bf16[1,512,3072]{2,1,0:T(8,128)(2,1)}) %all-gather.14.cloned.1.call-update) | async-done | bytes 3145744 | tf_op jit(solution)/shard_map/all_gather | solution.py:53
  104.9 0.0 all-gather.12.cloned.1.call-update
  105.0 0.0 all-gather.16.cloned.1.call-start
  105.0 5.8 %collective-permute-done = bf16[1,1,512,3072]{3,2,1,0:T(8,128)(2,1)S(1)} collective-permute-done((bf16[1,1,512,3072]{3,2,1,0:T(8,128)(2,1)}, bf16[1,1,512,3072]{3,2,1,0:T(8,128)(2,1)S(1)}, u32[]{:S(2)}, u32[]{:S(2)}) %collective-permute-start) | collective-permute-done | bytes 3145760 | tf_op jit(solution)/shard_map/ppermute | solution.py:20
  110.8 1.7 copy-done.1
  112.5 3.8 pad_maximum_fusion.1
  116.3 0.0 copy-start.3
  116.3 0.0 copy-start.2
  116.3 6.8 %fusion.7 = (bf16[1,2,1,512,3072]{4,3,1,2,0:T(8,128)(2,1)}, bf16[2,1,512,3072]{3,2,0,1:T(8,128)(2,1)}) fusion(bf16[2,1,1,512,3072]{4,3,2,1,0:T(8,128)(2,1)S(1)} %pad_maximum_fusion.1, pred[]{:T(512)S(6)} %eq.7), kind=kLoop, calls=%fused_computation.13 | loop fusion | flops 3145728 | bytes 18874368 | tf_op jit(solution)/shard_map/stack;reshape | solution.py:21
  123.1 1.5 collective-permute-start.1
  124.6 0.0 all-gather.16.cloned.1.call-update
  125.5 8.6 %all-gather = bf16[4,1,256]{2,1,0:T(2,128)(2,1)S(1)} all-gather(bf16[1,1,256]{2,1,0:T(2,128)(2,1)S(1)} %reshape.26), channel_id=1, replica_groups=mesh['row'=2,'col'=4,'tm'=4] {'tm'}, dimensions={0}, use_global_device_ids=true | all-gather | bytes 2560 | tf_op jit(solution)/shard_map/all_gather | solution.py:54
  134.1 13.3 %all-gather.1 = bf16[4,1,768]{2,1,0:T(2,128)(2,1)S(1)} all-gather(bf16[1,1,768]{2,1,0:T(2,128)(2,1)S(1)} %reshape.28), channel_id=1, replica_groups=mesh['row'=2,'col'=4,'tm'=4] {'tm'}, dimensions={0}, use_global_device_ids=true | all-gather | bytes 7680 | tf_op jit(solution)/shard_map/all_gather | solution.py:55
  147.4 0.0 all-gather.10.cloned.1.call-done
  147.5 49.3 %all-gather.12.cloned.1.call-done = bf16[4,512,1024]{2,1,0:T(8,128)(2,1)} async-done(((bf16[1,512,1024]{2,1,0:T(8,128)(2,1)}), bf16[4,512,1024]{2,1,0:T(8,128)(2,1)}) %all-gather.12.cloned.1.call-update) | async-done | bytes 4194320 | tf_op jit(solution)/shard_map/all_gather | solution.py:58
  196.7 11.7 %fusion.13 = f32[1024,2048]{1,0:T(8,128)} fusion(bf16[2048,1024]{1,0:T(8,128)(2,1)} %bitcast.55, bf16[1,1024,1024]{2,1,0:T(8,128)(2,1)} %all-gather.10.cloned.1.call-done, f32[1024]{0:T(1024)S(1)} %bitcast.54), kind=kOutput, calls=%fused_computation.18 | convolution fusion | flops 4298113024 | bytes 14684160 | tf_op jit(solution)/shard_map/dot_general | solution.py:39
  208.4 75.0 %collective-permute-done.1 = bf16[2,1,512,3072]{3,2,0,1:T(8,128)(2,1)} collective-permute-done((bf16[2,1,512,3072]{3,2,0,1:T(8,128)(2,1)}, bf16[2,1,512,3072]{3,2,0,1:T(8,128)(2,1)}, u32[]{:S(2)}, u32[]{:S(2)}) %collective-permute-start.1) | collective-permute-done | bytes 6291488 | tf_op jit(solution)/shard_map/ppermute | solution.py:20
  283.5 4.8 %pad_maximum_fusion = bf16[2,2,1,512,3072]{4,3,1,2,0:T(8,128)(2,1)S(1)} fusion(bf16[1,2,1,512,3072]{4,3,1,2,0:T(8,128)(2,1)} %bitcast.10, bf16[1,2,1,512,3072]{4,3,1,2,0:T(8,128)(2,1)S(1)} %bitcast.47), kind=kLoop, calls=%fused_computation.1 | loop fusion | flops 6291456 | bytes 25165824 | tf_op jit(solution)/shard_map/stack | solution.py:21
  288.2 8.3 %reverse_select_fusion = bf16[2,2,1,512,3072]{4,3,1,2,0:T(8,128)(2,1)} fusion(bf16[2,2,1,512,3072]{4,3,1,2,0:T(8,128)(2,1)S(1)} %pad_maximum_fusion, pred[]{:T(512)S(6)} %eq.6), kind=kLoop, calls=%fused_computation | loop fusion | flops 6291456 | bytes 25165824 | tf_op jit(solution)/shard_map/jit(_where)/select_n | solution.py:23
  296.5 20.6 %fusion.1 = bf16[2048,1024]{0,1:T(8,128)(2,1)} fusion(f32[1024,2048]{1,0:T(8,128)} %fusion.13, bf16[2048,3072]{1,0:T(8,128)(2,1)} %bitcast.51, bf16[1,1024,3072]{2,1,0:T(8,128)(2,1)} %all-gather.16.cloned.1.call-done, f32[3072]{0:T(1024)S(1)} %bitcast.53), kind=kOutput, calls=%fused_computation.6 | convolution fusion | flops 12900630528 | bytes 31469568 | tf_op jit(solution)/shard_map/dot_general | solution.py:39
  317.1 7.8 %broadcast_in_dim_reshape.3 = bf16[1,4,512,1024]{2,1,3,0:T(4,128)(2,1)} reshape(bf16[2048,1024]{0,1:T(8,128)(2,1)} %fusion.1) | data formatting | bytes 8388608 | tf_op jit(solution)/shard_map/broadcast_in_dim;reshape | solution.py:74
  324.9 10.0 %copy.14 = bf16[1,4,512,1024]{3,1,0,2:T(4,128)(2,1)} copy(bf16[1,4,512,1024]{2,1,3,0:T(4,128)(2,1)} %broadcast_in_dim_reshape.3) | data formatting | bytes 8388608 | tf_op jit(solution)/shard_map/broadcast_in_dim;reshape | solution.py:74
  335.0 96.6 %all_to_all.18 = bf16[1,4,512,1024]{3,1,0,2:T(4,128)(2,1)S(1)} all-to-all(bf16[1,4,512,1024]{3,1,0,2:T(4,128)(2,1)} %copy.14), channel_id=1, replica_groups=mesh['row'=2,'col'=4,'tm'=4] {'tm'}, dimensions={2} | all-to-all | bytes 8388608 | tf_op jit(solution)/shard_map/all_to_all | solution.py:74
  431.6 9.4 %convolution_bitcast_fusion = f32[4,4,128,1024]{3,0,2,1:T(4,128)S(1)} fusion(bf16[1,4,4,128,1024]{4,1,3,2,0:T(4,128)(2,1)S(1)} %bitcast.48, f32[4,4]{1,0:T(4,128)S(1)} %copy-done), kind=kOutput, calls=%fused_computation.11 | convolution fusion | flops 100663296 | bytes 12582976 | tf_op jit(solution)/shard_map/ft,tabc->fabc/dot_general | solution.py:71
  441.1 8.3 %copy.17 = f32[4,4,128,1024]{3,2,1,0:T(8,128)} copy(f32[4,4,128,1024]{3,0,2,1:T(4,128)S(1)} %convolution_bitcast_fusion) | data formatting | bytes 16777216 | tf_op jit(solution)/shard_map/ft,tabc->fabc/dot_general | solution.py:71
  (17 shorter events, 0.1 us)
Async XLA Ops:
  6.5 425.1 %copy-start = (f32[4,4]{1,0:T(4,128)S(1)}, f32[4,4]{1,0:T(4,128)}, u32[]{:S(2)}) copy-start(f32[4,4]{1,0:T(4,128)} %param.11) | copy-start | bytes 196
  6.5 35.0 %all-gather.8.cloned.1.call-start = ((), (), s32[]{:S(2)}) async-start(), calls=%async_computation.1 | async-start | bytes 1310720 | tf_op jit(solution)/shard_map/all_gather | solution.py:52
  7.3 97.7 %all-gather.14.cloned.1.call-start = ((), (), s32[]{:S(2)}) async-start(), calls=%async_computation.4 | async-start | bytes 3932160 | tf_op jit(solution)/shard_map/all_gather | solution.py:53
  8.0 139.4 %all-gather.10.cloned.1.call-start = ((), (), s32[]{:S(2)}) async-start(), calls=%async_computation.2 | async-start | bytes 3145728 | tf_op jit(solution)/shard_map/all_gather | solution.py:61
  41.6 155.1 %all-gather.12.cloned.1.call-start = ((), (), s32[]{:S(2)}) async-start(), calls=%async_computation.3 | async-start | bytes 5242880 | tf_op jit(solution)/shard_map/all_gather | solution.py:58
  104.9 5.9 %collective-permute-start = (bf16[1,1,512,3072]{3,2,1,0:T(8,128)(2,1)}, bf16[1,1,512,3072]{3,2,1,0:T(8,128)(2,1)S(1)}, u32[]{:S(2)}, u32[]{:S(2)}) collective-permute-start(bf16[1,1,512,3072]{3,2,1,0:T(8,128)(2,1)} %bitcast.49), channel_id=1, source_target_pairs={{0,4},{4,0},{8,12},{12,8},{1,5},{5,1},{9,13},{13,9},{2,6},{6,2},{1... | collective-permute-start | bytes 9437192 | tf_op jit(solution)/shard_map/ppermute | solution.py:20
  105.0 191.6 %all-gather.16.cloned.1.call-start = ((), (), s32[]{:S(2)}) async-start(), calls=%async_computation.5 | async-start | bytes 9437184 | tf_op jit(solution)/shard_map/all_gather | solution.py:61
  110.8 1.7 copy-start.1
  116.3 9.1 %copy-start.3 = (bf16[256]{0:T(256)(128)(2,1)S(1)}, bf16[256]{0:T(256)(128)(2,1)}, u32[]{:S(2)}) copy-start(bf16[256]{0:T(256)(128)(2,1)} %param.8) | copy-start | bytes 1540
  116.3 9.2 %copy-start.2 = (bf16[768]{0:T(1024)(128)(2,1)S(1)}, bf16[768]{0:T(1024)(128)(2,1)}, u32[]{:S(2)}) copy-start(bf16[768]{0:T(1024)(128)(2,1)} %param.9) | copy-start | bytes 4612
  123.1 160.4 %collective-permute-start.1 = (bf16[2,1,512,3072]{3,2,0,1:T(8,128)(2,1)}, bf16[2,1,512,3072]{3,2,0,1:T(8,128)(2,1)}, u32[]{:S(2)}, u32[]{:S(2)}) collective-permute-start(bf16[2,1,512,3072]{3,2,0,1:T(8,128)(2,1)} %get-tuple-element.6), channel_id=1, source_target_pairs={{0,8},{4,12},{8,0},{12,4},{1,9},{5,13},{9,1},{13,5},{2,10},{6,14},... | collective-permute-start | bytes 18874376 | tf_op jit(solution)/shard_map/ppermute | solution.py:20
  124.6 158.9 %slice-start = ((s8[6291456]{0:T(1024)(128)(4,1)}), s8[2097152]{0:T(1024)(128)(4,1)S(1)}, s32[]{:S(2)}) async-start(s8[6291456]{0:T(1024)(128)(4,1)} %bitcast.46), calls=%async_computation.6 | async-start | bytes 4194304
  196.7 86.8 %slice-start.1 = ((s8[6291456]{0:T(1024)(128)(4,1)}), s8[4194304]{0:T(1024)(128)(4,1)S(1)}, s32[]{:S(2)}) async-start(s8[6291456]{0:T(1024)(128)(4,1)} %bitcast.46), calls=%async_computation.7 | async-start | bytes 8388608
Sparse Core Ops, SparseCore 0:
  8.9 32.6 all-gather.7
  43.1 61.7 all-gather.13
  106.5 31.7 all-gather.9
  139.7 57.0 all-gather.11
  198.1 80.3 all-gather.15
